TPU v7x, 32 devices: a whole 2x2x4 slice. The times are simulated.
32 devices in a mesh: gx: 2 (over x), gy: 4 (over z), gz: 4 (over y, core).
Axes of the slice: x: 2, y: 2, z: 4, core: 2. Of those that a mesh axis runs over, the one named last changes fastest.
Arguments:
- schur: bfloat16 [2, 4, 4, 1024, 1024], P('gx', 'gy', 'gz'), may hold values from -0.2 to 2.7
- block_map: int32 [2, 4, 4, 26], P('gx', 'gy', 'gz'), may hold values from 0 to 7
- vectors: bfloat16 [2, 4, 4, 1024, 512], P('gx', 'gy', 'gz'), may hold values from -3 to 3
Outputs:
- assembled: bfloat16 [2, 4, 4, 1024, 512], P('gx', 'gy', 'gz')
- update: bfloat16 [2, 4, 4, 1024, 512], P('gx', 'gy', 'gz')
All inputs are finite; a program needn't handle non-finite values.
Results may differ from a plain program's by a relative error of at most 0.0056.
Values may be sent and summed in bfloat16 or wider, within the bound.
A program may use at most 64 MiB of HBM per device.

v0:
```python
import jax
import jax.numpy as jnp
from jax import lax
from jax.sharding import PartitionSpec as P

BLOCK = 128


def from_behind(value, axis, steps):
    count = lax.axis_size(axis)
    pairs = [(source, (source + steps) % count) for source in range(count)]
    return lax.ppermute(value, axis, pairs)


def directions():
    return [
        (a, b, c)
        for a in (-1, 0, 1)
        for b in (-1, 0, 1)
        for c in (-1, 0, 1)
        if (a, b, c) != (0, 0, 0)
    ]


def slot_number(along_x, along_y, along_z):
    return 9 * (along_x + 1) + 3 * (along_y + 1) + (along_z + 1)


def local(schur, block_map, vectors):
    offsets = directions()
    matrix = schur[0, 0, 0]
    right_side = vectors[0, 0, 0]
    block_links = block_map[0, 0, 0]
    order_size = matrix.shape[0]
    blocks = order_size // BLOCK
    product = jnp.dot(matrix, right_side, preferred_element_type=jnp.float32).astype(jnp.bfloat16)
    tile_grid = matrix.reshape(blocks, BLOCK, blocks, BLOCK)
    diagonal = jnp.stack([tile_grid[k, :, k, :] for k in range(blocks)])
    payload = jnp.concatenate([diagonal, product.reshape(blocks, BLOCK, -1)], axis=2)
    labels = jnp.arange(blocks, dtype=jnp.int32)
    centre = jnp.full((1,), -1, jnp.int32)
    links_grid = jnp.concatenate([block_links[:13], centre, block_links[13:]])
    send_chooser = (links_grid[:, None] == labels[None, :]).astype(jnp.bfloat16)
    outgoing = jnp.einsum(
        "sb,bij->sij", send_chooser, payload, preferred_element_type=jnp.float32
    ).astype(jnp.bfloat16)
    columns = lax.axis_size("gy")
    layers = lax.axis_size("gz")
    row_here = lax.axis_index("gy")
    layer_here = lax.axis_index("gz")
    plane_size = columns * layers
    received = jnp.zeros_like(outgoing)
    for along_x, along_y, along_z in offsets:
        target = slot_number(-along_x, -along_y, -along_z)
        stride = along_x * plane_size + along_y * layers + along_z
        moved = from_behind(outgoing[target], ("gx", "gy", "gz"), -stride)
        received = received.at[target].set(moved)
    alive_list = []
    for along_x in (-1, 0, 1):
        for along_y in (-1, 0, 1):
            for along_z in (-1, 0, 1):
                alive_list.append(
                    (row_here - along_y >= 0)
                    & (row_here - along_y < columns)
                    & (layer_here - along_z >= 0)
                    & (layer_here - along_z < layers)
                )
    alive = jnp.stack(alive_list).astype(jnp.bfloat16)
    receive_links = links_grid[::-1]
    weights = (receive_links[:, None] == labels[None, :]).astype(jnp.bfloat16) * alive[:, None]
    totals = payload.astype(jnp.float32) + jnp.einsum(
        "sb,sij->bij", weights, received, preferred_element_type=jnp.float32
    )
    counts = 1.0 + jnp.sum(weights.astype(jnp.float32), axis=0)
    coupling = totals[:, :, :BLOCK]
    summed = totals[:, :, BLOCK:]
    scaled = (
        jnp.einsum("bij,bjk->bik", coupling, summed, precision=lax.Precision.HIGHEST)
        / counts[:, None, None]
    ).astype(jnp.bfloat16)
    update = jnp.dot(
        matrix, scaled.reshape(order_size, -1), preferred_element_type=jnp.float32
    ).astype(jnp.bfloat16)
    assembled = summed.reshape(order_size, -1).astype(jnp.bfloat16)
    return (assembled[None, None, None], update[None, None, None])


def solution(mesh):
    placed = (
        P("gx", "gy", "gz", None, None),
        P("gx", "gy", "gz", None),
        P("gx", "gy", "gz", None, None),
    )
    return jax.shard_map(
        local,
        mesh=mesh,
        in_specs=placed,
        out_specs=(P("gx", "gy", "gz", None, None), P("gx", "gy", "gz", None, None)),
        check_vma=False,
    )
```

profile of v0, /device:TPU:17, one launch (start us, length us, event | category | flops | bytes accessed | tf_op | source)
XLA Modules:
  0.0 135.5 jit_solution(6638955325794243974)
XLA Ops:
  0.6 0.8 slice_bitcast_fusion.9
  1.9 3.0 %fusion.12 = bf16[1024,512]{1,0:T(8,128)(2,1)S(1)} fusion(bf16[1,1,1,1024,1024]{4,3,2,1,0:T(8,128)(2,1)} %param.55, bf16[1,1,1,1024,512]{4,3,2,1,0:T(8,128)(2,1)S(1)} %copy-done), kind=kOutput, calls=%fused_computation.11 | convolution fusion | flops 1074266112 | bytes 4194304 | tf_op jit(solution)/shard_map/dot_general | solution.py:36
  6.7 0.8 stack.22
  7.6 1.8 %convolution_convert_fusion = bf16[27,128,640]{2,0,1:T(8,128)(2,1)S(1)} fusion(bf16[8,128,512]{2,0,1:T(8,128)(2,1)S(1)} %copy.39, bf16[8,128,128]{2,0,1:T(8,128)(2,1)S(1)} %stack.22, s32[27]{0:T(128)S(1)} %pad_add_fusion), kind=kOutput, calls=%fused_computation.2 | convolution fusion | flops 40222936 | bytes 5734508 | tf_op jit(solution)/shard_map/sb,bij->sij/dot_general | solution.py:44
  9.4 2.3 %copy-done.1 = bf16[27,128,640]{2,0,1:T(8,128)(2,1)} copy-done((bf16[27,128,640]{2,0,1:T(8,128)(2,1)}, bf16[27,128,640]{2,0,1:T(8,128)(2,1)S(1)}, u32[]{:S(2)}) %copy-start.1) | copy-done | bytes 4423704
  11.7 1.8 %fusion.35 = (bf16[1,128,640]{2,0,1:T(2,128)(2,1)S(1)}, bf16[1,128,640]{2,0,1:T(2,128)(2,1)S(1)}, bf16[1,128,640]{2,0,1:T(2,128)(2,1)S(1)}, bf16[1,128,640]{2,0,...) fusion(bf16[27,128,640]{2,0,1:T(8,128)(2,1)S(1)} %convolution_c, ...), kind=kLoop, calls=%fused_computation.94 | loop fusion | bytes 2293760 | tf_op jit(solution)/shard_map/slice | solution.py:56
  13.5 0.7 copy.133
  14.2 3.7 %collective-permute-start = (bf16[128,640]{1,0:T(8,128)(2,1)}, bf16[128,640]{1,0:T(8,128)(2,1)S(1)}, u32[]{:S(2)}, u32[]{:S(2)}) collective-permute-start(bf16[128,640]{1,0:T(8,128)(2,1)} %bitcast.190), channel_id=1, source_target_pairs={{0,21},{1,22},{2,23},{3,24},{4,25},{5,26},{6,27},{7,28},{8,29},{9,... | collective-permute-start | bytes 491528 | tf_op jit(solution)/shard_map/ppermute | solution.py:12
  17.9 0.7 copy.132
  19.6 0.7 copy.130
  20.3 3.4 %collective-permute-start.3 = (bf16[128,640]{1,0:T(8,128)(2,1)}, bf16[128,640]{1,0:T(8,128)(2,1)}, u32[]{:S(2)}, u32[]{:S(2)}) collective-permute-start(bf16[128,640]{1,0:T(8,128)(2,1)} %bitcast.187), channel_id=1, source_target_pairs={{0,17},{1,18},{2,19},{3,20},{4,21},{5,22},{6,23},{7,24},{8,25},{9,... | collective-permute-start | bytes 491528 | tf_op jit(solution)/shard_map/ppermute | solution.py:12
  23.6 0.7 copy.129
  24.6 14.4 %fusion.34 = (bf16[1,128,640]{2,0,1:T(2,128)(2,1)}, bf16[1,128,640]{2,0,1:T(2,128)(2,1)}, bf16[1,128,640]{2,0,1:T(2,128)(2,1)}, bf16[1,128,640]{2,0,1:T(2,128)(2...) fusion(bf16[27,128,640]{2,0,1:T(8,128)(2,1)} %copy-done.1), kind=kLoop, calls=%fused_computation.93 | loop fusion | bytes 6225920 | tf_op jit(solution)/shard_map/slice | solution.py:56
  39.4 1.1 copy.108
  40.5 1.0 copy.109
  41.5 1.0 copy.110
  42.5 1.0 copy.111
  43.5 1.0 copy.112
  44.5 1.0 copy.113
  45.5 1.0 copy.114
  47.8 2.6 %collective-permute-start.6 = (bf16[128,640]{1,0:T(8,128)(2,1)S(1)}, bf16[128,640]{1,0:T(8,128)(2,1)S(1)}, u32[]{:S(2)}, u32[]{:S(2)}) collective-permute-start(bf16[128,640]{1,0:T(8,128)(2,1)S(1)} %bitcast.212), channel_id=1, source_target_pairs={{0,13},{1,14},{2,15},{3,16},{4,17},{5,18},{6,19},{7,20},{8,21},{9,... | collective-permute-start | bytes 491528 | tf_op jit(solution)/shard_map/ppermute | solution.py:12
  50.4 0.9 bitcast_dynamic-update-slice_fusion.24
  51.4 2.4 %collective-permute-start.7 = (bf16[128,640]{1,0:T(8,128)(2,1)S(1)}, bf16[128,640]{1,0:T(8,128)(2,1)S(1)}, u32[]{:S(2)}, u32[]{:S(2)}) collective-permute-start(bf16[128,640]{1,0:T(8,128)(2,1)S(1)} %bitcast.216), channel_id=1, source_target_pairs={{0,12},{1,13},{2,14},{3,15},{4,16},{5,17},{6,18},{7,19},{8,20},{9,... | collective-permute-start | bytes 491528 | tf_op jit(solution)/shard_map/ppermute | solution.py:12
  53.8 0.9 bitcast_dynamic-update-slice_fusion.23
  54.8 1.2 collective-permute-start.8
  56.0 0.9 bitcast_dynamic-update-slice_fusion.22
  56.9 2.5 %collective-permute-start.9 = (bf16[128,640]{1,0:T(8,128)(2,1)S(1)}, bf16[128,640]{1,0:T(8,128)(2,1)S(1)}, u32[]{:S(2)}, u32[]{:S(2)}) collective-permute-start(bf16[128,640]{1,0:T(8,128)(2,1)S(1)} %bitcast.213), channel_id=1, source_target_pairs={{0,5},{1,6},{2,7},{3,8},{4,9},{5,10},{6,11},{7,12},{8,13},{9,14},{... | collective-permute-start | bytes 491528 | tf_op jit(solution)/shard_map/ppermute | solution.py:12
  59.4 0.9 bitcast_dynamic-update-slice_fusion.21
  60.3 3.4 %collective-permute-done.5 = bf16[128,640]{1,0:T(8,128)(2,1)S(1)} collective-permute-done((bf16[128,640]{1,0:T(8,128)(2,1)S(1)}, bf16[128,640]{1,0:T(8,128)(2,1)S(1)}, u32[]{:S(2)}, u32[]{:S(2)}) %collective-permute-start.5) | collective-permute-done | bytes 163872 | tf_op jit(solution)/shard_map/ppermute | solution.py:12
  63.7 4.0 %collective-permute-start.11 = (bf16[128,640]{1,0:T(8,128)(2,1)S(1)}, bf16[128,640]{1,0:T(8,128)(2,1)S(1)}, u32[]{:S(2)}, u32[]{:S(2)}) collective-permute-start(bf16[128,640]{1,0:T(8,128)(2,1)S(1)} %bitcast.210), channel_id=1, source_target_pairs={{0,3},{1,4},{2,5},{3,6},{4,7},{5,8},{6,9},{7,10},{8,11},{9,12},{10... | collective-permute-start | bytes 491528 | tf_op jit(solution)/shard_map/ppermute | solution.py:12
  68.5 3.9 %collective-permute-done.9 = bf16[128,640]{1,0:T(8,128)(2,1)S(1)} collective-permute-done((bf16[128,640]{1,0:T(8,128)(2,1)S(1)}, bf16[128,640]{1,0:T(8,128)(2,1)S(1)}, u32[]{:S(2)}, u32[]{:S(2)}) %collective-permute-start.9) | collective-permute-done | bytes 163872 | tf_op jit(solution)/shard_map/ppermute | solution.py:12
  72.3 3.3 %collective-permute-start.14 = (bf16[128,640]{1,0:T(8,128)(2,1)S(1)}, bf16[128,640]{1,0:T(8,128)(2,1)S(1)}, u32[]{:S(2)}, u32[]{:S(2)}) collective-permute-start(bf16[128,640]{1,0:T(8,128)(2,1)S(1)} %bitcast.207), channel_id=1, source_target_pairs={{0,29},{1,30},{2,31},{3,0},{4,1},{5,2},{6,3},{7,4},{8,5},{9,6},{10... | collective-permute-start | bytes 491528 | tf_op jit(solution)/shard_map/ppermute | solution.py:12
  75.8 6.4 %collective-permute-start.16 = (bf16[128,640]{1,0:T(8,128)(2,1)S(1)}, bf16[128,640]{1,0:T(8,128)(2,1)S(1)}, u32[]{:S(2)}, u32[]{:S(2)}) collective-permute-start(bf16[128,640]{1,0:T(8,128)(2,1)S(1)} %bitcast.205), channel_id=1, source_target_pairs={{0,27},{1,28},{2,29},{3,30},{4,31},{5,0},{6,1},{7,2},{8,3},{9,4},{... | collective-permute-start | bytes 491528 | tf_op jit(solution)/shard_map/ppermute | solution.py:12
  82.5 3.4 %collective-permute-start.18 = (bf16[128,640]{1,0:T(8,128)(2,1)S(1)}, bf16[128,640]{1,0:T(8,128)(2,1)S(1)}, u32[]{:S(2)}, u32[]{:S(2)}) collective-permute-start(bf16[128,640]{1,0:T(8,128)(2,1)S(1)} %bitcast.203), channel_id=1, source_target_pairs={{0,20},{1,21},{2,22},{3,23},{4,24},{5,25},{6,26},{7,27},{8,28},{9,... | collective-permute-start | bytes 491528 | tf_op jit(solution)/shard_map/ppermute | solution.py:12
  86.1 2.4 %collective-permute-start.19 = (bf16[128,640]{1,0:T(8,128)(2,1)S(1)}, bf16[128,640]{1,0:T(8,128)(2,1)S(1)}, u32[]{:S(2)}, u32[]{:S(2)}) collective-permute-start(bf16[128,640]{1,0:T(8,128)(2,1)S(1)} %bitcast.202), channel_id=1, source_target_pairs={{0,19},{1,20},{2,21},{3,22},{4,23},{5,24},{6,25},{7,26},{8,27},{9,... | collective-permute-start | bytes 491528 | tf_op jit(solution)/shard_map/ppermute | solution.py:12
  88.5 5.0 %collective-permute-start.20 = (bf16[128,640]{1,0:T(8,128)(2,1)S(1)}, bf16[128,640]{1,0:T(8,128)(2,1)S(1)}, u32[]{:S(2)}, u32[]{:S(2)}) collective-permute-start(bf16[128,640]{1,0:T(8,128)(2,1)S(1)} %bitcast.201), channel_id=1, source_target_pairs={{0,17},{1,18},{2,19},{3,20},{4,21},{5,22},{6,23},{7,24},{8,25},{9,... | collective-permute-start | bytes 491528 | tf_op jit(solution)/shard_map/ppermute | solution.py:12
  93.6 1.0 collective-permute-start.21
  94.6 7.5 %collective-permute-done.17 = bf16[128,640]{1,0:T(8,128)(2,1)S(1)} collective-permute-done((bf16[128,640]{1,0:T(8,128)(2,1)S(1)}, bf16[128,640]{1,0:T(8,128)(2,1)S(1)}, u32[]{:S(2)}, u32[]{:S(2)}) %collective-permute-start.17) | collective-permute-done | bytes 163872 | tf_op jit(solution)/shard_map/ppermute | solution.py:12
  103.1 0.9 collective-permute-done.19
  104.0 5.2 %collective-permute-start.24 = (bf16[128,640]{1,0:T(8,128)(2,1)S(1)}, bf16[128,640]{1,0:T(8,128)(2,1)S(1)}, u32[]{:S(2)}, u32[]{:S(2)}) collective-permute-start(bf16[128,640]{1,0:T(8,128)(2,1)S(1)} %bitcast.197), channel_id=1, source_target_pairs={{0,12},{1,13},{2,14},{3,15},{4,16},{5,17},{6,18},{7,19},{8,20},{9,... | collective-permute-start | bytes 491528 | tf_op jit(solution)/shard_map/ppermute | solution.py:12
  109.2 8.3 %collective-permute-done.20 = bf16[128,640]{1,0:T(8,128)(2,1)S(1)} collective-permute-done((bf16[128,640]{1,0:T(8,128)(2,1)S(1)}, bf16[128,640]{1,0:T(8,128)(2,1)S(1)}, u32[]{:S(2)}, u32[]{:S(2)}) %collective-permute-start.20) | collective-permute-done | bytes 163872 | tf_op jit(solution)/shard_map/ppermute | solution.py:12
  117.5 4.9 %collective-permute-done.21 = bf16[128,640]{1,0:T(8,128)(2,1)S(1)} collective-permute-done((bf16[128,640]{1,0:T(8,128)(2,1)S(1)}, bf16[128,640]{1,0:T(8,128)(2,1)S(1)}, u32[]{:S(2)}, u32[]{:S(2)}) %collective-permute-start.21) | collective-permute-done | bytes 163872 | tf_op jit(solution)/shard_map/ppermute | solution.py:12
  122.7 2.4 %collective-permute-done.25 = bf16[128,640]{1,0:T(8,128)(2,1)S(1)} collective-permute-done((bf16[128,640]{1,0:T(8,128)(2,1)S(1)}, bf16[128,640]{1,0:T(8,128)(2,1)S(1)}, u32[]{:S(2)}, u32[]{:S(2)}) %collective-permute-start.25) | collective-permute-done | bytes 163872 | tf_op jit(solution)/shard_map/ppermute | solution.py:12
  125.1 3.0 %convert_add_fusion = f32[8,128,640]{2,0,1:T(8,128)S(1)} fusion(bf16[27,128,640]{2,1,0:T(8,128)(2,1)S(1)} %bitcast_dynamic-update-slice_fusion, bf16[8,128,512]{2,0,1:T(8,128)(2,1)S(1)} %copy.39, bf16[8,128,128]{2,0,1:T(8,128)(2,1)S(1)} %stack.22, s32[27]{0:T(128)S(1)} %rev.3, bf16[27]{0:T(256)(128)(2,1)S(1)} %convert_element_type.45), kind=kOutput, calls=%fused_computation.3 | convolution fusion | flops 38666672 | bytes 8356002 | tf_op jit(solution)/shard_map/sb,sij->bij/dot_general | solution.py:71
  128.5 3.0 %divide_convert_fusion = bf16[8,128,512]{2,1,0:T(8,128)(2,1)S(1)} fusion(f32[8,128,512]{2,0,1:T(8,128)S(1)} %slice.713, f32[8]{0:T(128)S(1)} %broadcast_add_fusion, f32[8,128,128]{2,0,1:T(8,128)S(1)} %slice.714), kind=kOutput, calls=%fused_computation.10 | convolution fusion | flops 806354944 | bytes 3670048 | tf_op jit(solution)/shard_map/bij,bjk->bik/dot_general | solution.py:78
  131.6 1.3 fusion.18
  132.9 1.3 copy.44
  134.2 1.3 copy.41
  (109 shorter events, 8.0 us)
Async XLA Ops:
  0.6 1.3 copy-start
  1.9 3.6 %copy-start.2 = (bf16[1,1,1,1024,1024]{4,3,2,1,0:T(8,128)(2,1)S(1)}, bf16[1,1,1,1024,1024]{4,3,2,1,0:T(8,128)(2,1)}, u32[]{:S(2)}) copy-start(bf16[1,1,1,1024,1024]{4,3,2,1,0:T(8,128)(2,1)} %param.55) | copy-start | bytes 6291460
  9.4 2.3 %copy-start.1 = (bf16[27,128,640]{2,0,1:T(8,128)(2,1)}, bf16[27,128,640]{2,0,1:T(8,128)(2,1)S(1)}, u32[]{:S(2)}) copy-start(bf16[27,128,640]{2,0,1:T(8,128)(2,1)S(1)} %convolution_convert_fusion) | copy-start | bytes 13271044
  14.2 32.9 %collective-permute-start = (bf16[128,640]{1,0:T(8,128)(2,1)}, bf16[128,640]{1,0:T(8,128)(2,1)S(1)}, u32[]{:S(2)}, u32[]{:S(2)}) collective-permute-start(bf16[128,640]{1,0:T(8,128)(2,1)} %bitcast.190), channel_id=1, source_target_pairs={{0,21},{1,22},{2,23},{3,24},{4,25},{5,26},{6,27},{7,28},{8,29},{9,... | collective-permute-start | bytes 491528 | tf_op jit(solution)/shard_map/ppermute | solution.py:12
  18.6 29.2 %collective-permute-start.1 = (bf16[128,640]{1,0:T(8,128)(2,1)}, bf16[128,640]{1,0:T(8,128)(2,1)}, u32[]{:S(2)}, u32[]{:S(2)}) collective-permute-start(bf16[128,640]{1,0:T(8,128)(2,1)} %bitcast.189), channel_id=1, source_target_pairs={{0,20},{1,21},{2,22},{3,23},{4,24},{5,25},{6,26},{7,27},{8,28},{9,... | collective-permute-start | bytes 491528 | tf_op jit(solution)/shard_map/ppermute | solution.py:12
  19.3 32.1 %collective-permute-start.2 = (bf16[128,640]{1,0:T(8,128)(2,1)}, bf16[128,640]{1,0:T(8,128)(2,1)}, u32[]{:S(2)}, u32[]{:S(2)}) collective-permute-start(bf16[128,640]{1,0:T(8,128)(2,1)} %bitcast.188), channel_id=1, source_target_pairs={{0,19},{1,20},{2,21},{3,22},{4,23},{5,24},{6,25},{7,26},{8,27},{9,... | collective-permute-start | bytes 491528 | tf_op jit(solution)/shard_map/ppermute | solution.py:12
  20.3 34.5 %collective-permute-start.3 = (bf16[128,640]{1,0:T(8,128)(2,1)}, bf16[128,640]{1,0:T(8,128)(2,1)}, u32[]{:S(2)}, u32[]{:S(2)}) collective-permute-start(bf16[128,640]{1,0:T(8,128)(2,1)} %bitcast.187), channel_id=1, source_target_pairs={{0,17},{1,18},{2,19},{3,20},{4,21},{5,22},{6,23},{7,24},{8,25},{9,... | collective-permute-start | bytes 491528 | tf_op jit(solution)/shard_map/ppermute | solution.py:12
  24.3 32.6 %collective-permute-start.4 = (bf16[128,640]{1,0:T(8,128)(2,1)}, bf16[128,640]{1,0:T(8,128)(2,1)}, u32[]{:S(2)}, u32[]{:S(2)}) collective-permute-start(bf16[128,640]{1,0:T(8,128)(2,1)} %bitcast.186), channel_id=1, source_target_pairs={{0,16},{1,17},{2,18},{3,19},{4,20},{5,21},{6,22},{7,23},{8,24},{9,... | collective-permute-start | bytes 491528 | tf_op jit(solution)/shard_map/ppermute | solution.py:12
  39.2 7.3 %copy-start.14 = (bf16[1,128,640]{2,0,1:T(2,128)(2,1)S(1)}, bf16[1,128,640]{2,0,1:T(2,128)(2,1)}, u32[]{:S(2)}) copy-start(bf16[1,128,640]{2,0,1:T(2,128)(2,1)} %get-tuple-element.327) | copy-start | bytes 491524
  39.2 7.4 %copy-start.13 = (bf16[1,128,640]{2,0,1:T(2,128)(2,1)S(1)}, bf16[1,128,640]{2,0,1:T(2,128)(2,1)}, u32[]{:S(2)}) copy-start(bf16[1,128,640]{2,0,1:T(2,128)(2,1)} %get-tuple-element.328) | copy-start | bytes 491524
  39.2 7.4 %copy-start.12 = (bf16[1,128,640]{2,0,1:T(2,128)(2,1)S(1)}, bf16[1,128,640]{2,0,1:T(2,128)(2,1)}, u32[]{:S(2)}) copy-start(bf16[1,128,640]{2,0,1:T(2,128)(2,1)} %get-tuple-element.329) | copy-start | bytes 491524
  39.2 7.4 %copy-start.11 = (bf16[1,128,640]{2,0,1:T(2,128)(2,1)S(1)}, bf16[1,128,640]{2,0,1:T(2,128)(2,1)}, u32[]{:S(2)}) copy-start(bf16[1,128,640]{2,0,1:T(2,128)(2,1)} %get-tuple-element.330) | copy-start | bytes 491524
  39.2 7.5 %copy-start.10 = (bf16[1,128,640]{2,0,1:T(2,128)(2,1)S(1)}, bf16[1,128,640]{2,0,1:T(2,128)(2,1)}, u32[]{:S(2)}) copy-start(bf16[1,128,640]{2,0,1:T(2,128)(2,1)} %get-tuple-element.331) | copy-start | bytes 491524
  39.3 7.5 %copy-start.9 = (bf16[1,128,640]{2,0,1:T(2,128)(2,1)S(1)}, bf16[1,128,640]{2,0,1:T(2,128)(2,1)}, u32[]{:S(2)}) copy-start(bf16[1,128,640]{2,0,1:T(2,128)(2,1)} %get-tuple-element.332) | copy-start | bytes 491524
  39.3 7.5 %copy-start.8 = (bf16[1,128,640]{2,0,1:T(2,128)(2,1)S(1)}, bf16[1,128,640]{2,0,1:T(2,128)(2,1)}, u32[]{:S(2)}) copy-start(bf16[1,128,640]{2,0,1:T(2,128)(2,1)} %get-tuple-element.333) | copy-start | bytes 491524
  39.3 7.6 %copy-start.7 = (bf16[1,128,640]{2,0,1:T(2,128)(2,1)S(1)}, bf16[1,128,640]{2,0,1:T(2,128)(2,1)}, u32[]{:S(2)}) copy-start(bf16[1,128,640]{2,0,1:T(2,128)(2,1)} %get-tuple-element.334) | copy-start | bytes 491524
  39.3 7.6 %copy-start.6 = (bf16[1,128,640]{2,0,1:T(2,128)(2,1)S(1)}, bf16[1,128,640]{2,0,1:T(2,128)(2,1)}, u32[]{:S(2)}) copy-start(bf16[1,128,640]{2,0,1:T(2,128)(2,1)} %get-tuple-element.335) | copy-start | bytes 491524
  39.3 7.6 %copy-start.5 = (bf16[1,128,640]{2,0,1:T(2,128)(2,1)S(1)}, bf16[1,128,640]{2,0,1:T(2,128)(2,1)}, u32[]{:S(2)}) copy-start(bf16[1,128,640]{2,0,1:T(2,128)(2,1)} %get-tuple-element.336) | copy-start | bytes 491524
  39.4 7.6 %copy-start.4 = (bf16[1,128,640]{2,0,1:T(2,128)(2,1)S(1)}, bf16[1,128,640]{2,0,1:T(2,128)(2,1)}, u32[]{:S(2)}) copy-start(bf16[1,128,640]{2,0,1:T(2,128)(2,1)} %get-tuple-element.337) | copy-start | bytes 491524
  47.2 16.5 %collective-permute-start.5 = (bf16[128,640]{1,0:T(8,128)(2,1)S(1)}, bf16[128,640]{1,0:T(8,128)(2,1)S(1)}, u32[]{:S(2)}, u32[]{:S(2)}) collective-permute-start(bf16[128,640]{1,0:T(8,128)(2,1)S(1)} %bitcast.214), channel_id=1, source_target_pairs={{0,15},{1,16},{2,17},{3,18},{4,19},{5,20},{6,21},{7,22},{8,23},{9,... | collective-permute-start | bytes 491528 | tf_op jit(solution)/shard_map/ppermute | solution.py:12
  47.8 15.9 %collective-permute-start.6 = (bf16[128,640]{1,0:T(8,128)(2,1)S(1)}, bf16[128,640]{1,0:T(8,128)(2,1)S(1)}, u32[]{:S(2)}, u32[]{:S(2)}) collective-permute-start(bf16[128,640]{1,0:T(8,128)(2,1)S(1)} %bitcast.212), channel_id=1, source_target_pairs={{0,13},{1,14},{2,15},{3,16},{4,17},{5,18},{6,19},{7,20},{8,21},{9,... | collective-permute-start | bytes 491528 | tf_op jit(solution)/shard_map/ppermute | solution.py:12
  51.4 16.4 %collective-permute-start.7 = (bf16[128,640]{1,0:T(8,128)(2,1)S(1)}, bf16[128,640]{1,0:T(8,128)(2,1)S(1)}, u32[]{:S(2)}, u32[]{:S(2)}) collective-permute-start(bf16[128,640]{1,0:T(8,128)(2,1)S(1)} %bitcast.216), channel_id=1, source_target_pairs={{0,12},{1,13},{2,14},{3,15},{4,16},{5,17},{6,18},{7,19},{8,20},{9,... | collective-permute-start | bytes 491528 | tf_op jit(solution)/shard_map/ppermute | solution.py:12
  54.8 13.1 %collective-permute-start.8 = (bf16[128,640]{1,0:T(8,128)(2,1)S(1)}, bf16[128,640]{1,0:T(8,128)(2,1)S(1)}, u32[]{:S(2)}, u32[]{:S(2)}) collective-permute-start(bf16[128,640]{1,0:T(8,128)(2,1)S(1)} %bitcast.215), channel_id=1, source_target_pairs={{0,11},{1,12},{2,13},{3,14},{4,15},{5,16},{6,17},{7,18},{8,19},{9,... | collective-permute-start | bytes 491528 | tf_op jit(solution)/shard_map/ppermute | solution.py:12
  56.9 15.4 %collective-permute-start.9 = (bf16[128,640]{1,0:T(8,128)(2,1)S(1)}, bf16[128,640]{1,0:T(8,128)(2,1)S(1)}, u32[]{:S(2)}, u32[]{:S(2)}) collective-permute-start(bf16[128,640]{1,0:T(8,128)(2,1)S(1)} %bitcast.213), channel_id=1, source_target_pairs={{0,5},{1,6},{2,7},{3,8},{4,9},{5,10},{6,11},{7,12},{8,13},{9,14},{... | collective-permute-start | bytes 491528 | tf_op jit(solution)/shard_map/ppermute | solution.py:12
  63.7 12.0 %collective-permute-start.10 = (bf16[128,640]{1,0:T(8,128)(2,1)S(1)}, bf16[128,640]{1,0:T(8,128)(2,1)S(1)}, u32[]{:S(2)}, u32[]{:S(2)}) collective-permute-start(bf16[128,640]{1,0:T(8,128)(2,1)S(1)} %bitcast.211), channel_id=1, source_target_pairs={{0,4},{1,5},{2,6},{3,7},{4,8},{5,9},{6,10},{7,11},{8,12},{9,13},{1... | collective-permute-start | bytes 491528 | tf_op jit(solution)/shard_map/ppermute | solution.py:12
  63.7 12.1 %collective-permute-start.11 = (bf16[128,640]{1,0:T(8,128)(2,1)S(1)}, bf16[128,640]{1,0:T(8,128)(2,1)S(1)}, u32[]{:S(2)}, u32[]{:S(2)}) collective-permute-start(bf16[128,640]{1,0:T(8,128)(2,1)S(1)} %bitcast.210), channel_id=1, source_target_pairs={{0,3},{1,4},{2,5},{3,6},{4,7},{5,8},{6,9},{7,10},{8,11},{9,12},{10... | collective-permute-start | bytes 491528 | tf_op jit(solution)/shard_map/ppermute | solution.py:12
  67.8 14.4 %collective-permute-start.12 = (bf16[128,640]{1,0:T(8,128)(2,1)S(1)}, bf16[128,640]{1,0:T(8,128)(2,1)S(1)}, u32[]{:S(2)}, u32[]{:S(2)}) collective-permute-start(bf16[128,640]{1,0:T(8,128)(2,1)S(1)} %bitcast.209), channel_id=1, source_target_pairs={{0,1},{1,2},{2,3},{3,4},{4,5},{5,6},{6,7},{7,8},{8,9},{9,10},{10,1... | collective-permute-start | bytes 491528 | tf_op jit(solution)/shard_map/ppermute | solution.py:12
  67.9 14.6 %collective-permute-start.13 = (bf16[128,640]{1,0:T(8,128)(2,1)S(1)}, bf16[128,640]{1,0:T(8,128)(2,1)S(1)}, u32[]{:S(2)}, u32[]{:S(2)}) collective-permute-start(bf16[128,640]{1,0:T(8,128)(2,1)S(1)} %bitcast.208), channel_id=1, source_target_pairs={{0,31},{1,0},{2,1},{3,2},{4,3},{5,4},{6,5},{7,6},{8,7},{9,8},{10,9... | collective-permute-start | bytes 491528 | tf_op jit(solution)/shard_map/ppermute | solution.py:12
  72.3 13.8 %collective-permute-start.14 = (bf16[128,640]{1,0:T(8,128)(2,1)S(1)}, bf16[128,640]{1,0:T(8,128)(2,1)S(1)}, u32[]{:S(2)}, u32[]{:S(2)}) collective-permute-start(bf16[128,640]{1,0:T(8,128)(2,1)S(1)} %bitcast.207), channel_id=1, source_target_pairs={{0,29},{1,30},{2,31},{3,0},{4,1},{5,2},{6,3},{7,4},{8,5},{9,6},{10... | collective-permute-start | bytes 491528 | tf_op jit(solution)/shard_map/ppermute | solution.py:12
  75.7 12.9 %collective-permute-start.15 = (bf16[128,640]{1,0:T(8,128)(2,1)S(1)}, bf16[128,640]{1,0:T(8,128)(2,1)S(1)}, u32[]{:S(2)}, u32[]{:S(2)}) collective-permute-start(bf16[128,640]{1,0:T(8,128)(2,1)S(1)} %bitcast.206), channel_id=1, source_target_pairs={{0,28},{1,29},{2,30},{3,31},{4,0},{5,1},{6,2},{7,3},{8,4},{9,5},{1... | collective-permute-start | bytes 491528 | tf_op jit(solution)/shard_map/ppermute | solution.py:12
  75.8 17.8 %collective-permute-start.16 = (bf16[128,640]{1,0:T(8,128)(2,1)S(1)}, bf16[128,640]{1,0:T(8,128)(2,1)S(1)}, u32[]{:S(2)}, u32[]{:S(2)}) collective-permute-start(bf16[128,640]{1,0:T(8,128)(2,1)S(1)} %bitcast.205), channel_id=1, source_target_pairs={{0,27},{1,28},{2,29},{3,30},{4,31},{5,0},{6,1},{7,2},{8,3},{9,4},{... | collective-permute-start | bytes 491528 | tf_op jit(solution)/shard_map/ppermute | solution.py:12
  82.2 19.9 %collective-permute-start.17 = (bf16[128,640]{1,0:T(8,128)(2,1)S(1)}, bf16[128,640]{1,0:T(8,128)(2,1)S(1)}, u32[]{:S(2)}, u32[]{:S(2)}) collective-permute-start(bf16[128,640]{1,0:T(8,128)(2,1)S(1)} %bitcast.204), channel_id=1, source_target_pairs={{0,21},{1,22},{2,23},{3,24},{4,25},{5,26},{6,27},{7,28},{8,29},{9,... | collective-permute-start | bytes 491528 | tf_op jit(solution)/shard_map/ppermute | solution.py:12
  82.5 20.1 %collective-permute-start.18 = (bf16[128,640]{1,0:T(8,128)(2,1)S(1)}, bf16[128,640]{1,0:T(8,128)(2,1)S(1)}, u32[]{:S(2)}, u32[]{:S(2)}) collective-permute-start(bf16[128,640]{1,0:T(8,128)(2,1)S(1)} %bitcast.203), channel_id=1, source_target_pairs={{0,20},{1,21},{2,22},{3,23},{4,24},{5,25},{6,26},{7,27},{8,28},{9,... | collective-permute-start | bytes 491528 | tf_op jit(solution)/shard_map/ppermute | solution.py:12
  86.1 17.9 %collective-permute-start.19 = (bf16[128,640]{1,0:T(8,128)(2,1)S(1)}, bf16[128,640]{1,0:T(8,128)(2,1)S(1)}, u32[]{:S(2)}, u32[]{:S(2)}) collective-permute-start(bf16[128,640]{1,0:T(8,128)(2,1)S(1)} %bitcast.202), channel_id=1, source_target_pairs={{0,19},{1,20},{2,21},{3,22},{4,23},{5,24},{6,25},{7,26},{8,27},{9,... | collective-permute-start | bytes 491528 | tf_op jit(solution)/shard_map/ppermute | solution.py:12
  88.5 28.9 %collective-permute-start.20 = (bf16[128,640]{1,0:T(8,128)(2,1)S(1)}, bf16[128,640]{1,0:T(8,128)(2,1)S(1)}, u32[]{:S(2)}, u32[]{:S(2)}) collective-permute-start(bf16[128,640]{1,0:T(8,128)(2,1)S(1)} %bitcast.201), channel_id=1, source_target_pairs={{0,17},{1,18},{2,19},{3,20},{4,21},{5,22},{6,23},{7,24},{8,25},{9,... | collective-permute-start | bytes 491528 | tf_op jit(solution)/shard_map/ppermute | solution.py:12
  93.6 28.7 %collective-permute-start.21 = (bf16[128,640]{1,0:T(8,128)(2,1)S(1)}, bf16[128,640]{1,0:T(8,128)(2,1)S(1)}, u32[]{:S(2)}, u32[]{:S(2)}) collective-permute-start(bf16[128,640]{1,0:T(8,128)(2,1)S(1)} %bitcast.200), channel_id=1, source_target_pairs={{0,16},{1,17},{2,18},{3,19},{4,20},{5,21},{6,22},{7,23},{8,24},{9,... | collective-permute-start | bytes 491528 | tf_op jit(solution)/shard_map/ppermute | solution.py:12
  102.1 20.5 %collective-permute-start.22 = (bf16[128,640]{1,0:T(8,128)(2,1)S(1)}, bf16[128,640]{1,0:T(8,128)(2,1)S(1)}, u32[]{:S(2)}, u32[]{:S(2)}) collective-permute-start(bf16[128,640]{1,0:T(8,128)(2,1)S(1)} %bitcast.199), channel_id=1, source_target_pairs={{0,15},{1,16},{2,17},{3,18},{4,19},{5,20},{6,21},{7,22},{8,23},{9,... | collective-permute-start | bytes 491528 | tf_op jit(solution)/shard_map/ppermute | solution.py:12
  102.6 20.0 %collective-permute-start.23 = (bf16[128,640]{1,0:T(8,128)(2,1)S(1)}, bf16[128,640]{1,0:T(8,128)(2,1)S(1)}, u32[]{:S(2)}, u32[]{:S(2)}) collective-permute-start(bf16[128,640]{1,0:T(8,128)(2,1)S(1)} %bitcast.198), channel_id=1, source_target_pairs={{0,13},{1,14},{2,15},{3,16},{4,17},{5,18},{6,19},{7,20},{8,21},{9,... | collective-permute-start | bytes 491528 | tf_op jit(solution)/shard_map/ppermute | solution.py:12
  104.0 18.7 %collective-permute-start.24 = (bf16[128,640]{1,0:T(8,128)(2,1)S(1)}, bf16[128,640]{1,0:T(8,128)(2,1)S(1)}, u32[]{:S(2)}, u32[]{:S(2)}) collective-permute-start(bf16[128,640]{1,0:T(8,128)(2,1)S(1)} %bitcast.197), channel_id=1, source_target_pairs={{0,12},{1,13},{2,14},{3,15},{4,16},{5,17},{6,18},{7,19},{8,20},{9,... | collective-permute-start | bytes 491528 | tf_op jit(solution)/shard_map/ppermute | solution.py:12
  117.4 7.6 %collective-permute-start.25 = (bf16[128,640]{1,0:T(8,128)(2,1)S(1)}, bf16[128,640]{1,0:T(8,128)(2,1)S(1)}, u32[]{:S(2)}, u32[]{:S(2)}) collective-permute-start(bf16[128,640]{1,0:T(8,128)(2,1)S(1)} %bitcast.196), channel_id=1, source_target_pairs={{0,11},{1,12},{2,13},{3,14},{4,15},{5,16},{6,17},{7,18},{8,19},{9,... | collective-permute-start | bytes 491528 | tf_op jit(solution)/shard_map/ppermute | solution.py:12
  128.5 3.1 %copy-start.3 = (bf16[1,1,1,1024,1024]{4,3,2,1,0:T(8,128)(2,1)S(1)}, bf16[1,1,1,1024,1024]{4,3,2,1,0:T(8,128)(2,1)}, u32[]{:S(2)}) copy-start(bf16[1,1,1,1024,1024]{4,3,2,1,0:T(8,128)(2,1)} %param.55) | copy-start | bytes 6291460
where the time goes:
time: 136 us; the launch traced here: 135 us
  starting transfers between devices  48.6 us (36%)
  local copies, waits for them, and re-layouts  41.3 us (30%)
  waiting for transfers between devices  31.9 us (23%)
  matrix products  12.1 us (9%)
    ppermute x26, starting transfers between devices, from_behind(): return lax.ppermute(value, axis, pairs)  48.6 us
    ppermute x26, waiting for transfers between devices, from_behind(): return lax.ppermute(value, axis, pairs)  31.9 us
    slice x2, local copies, waits for them, and re-layouts, local(): moved = from_behind(outgoing[target], ('gx', 'gy', 'gz'), -stride)  16.2 us
    unnamed x58, local copies, waits for them, and re-layouts  15.6 us
    scatter x26, local copies, waits for them, and re-layouts, local(): received = received.at[target].set(moved)  4.78 us
    dot_general x1, matrix products, local(): jnp.einsum('bij,bjk->bik', coupling, summed, precision=lax.Precision.HIGH...  3.04 us
    dot_general x1, matrix products, local(): jnp.dot(matrix, right_side, preferred_element_type=jnp.float32)  2.98 us
    dot_general x1, matrix products, local(): jnp.einsum('sb,sij->bij', weights, received, preferred_element_type=jnp.f...  2.96 us
  transfers between devices with their start and end apart: 26, of which 10 were waited for; matrix products, arithmetic and copies ran while one was open for 22% of the time, Pallas kernels for 0%

commit v1 on v0

v1 whole, which is shorter than its diff:
```python
import functools

import jax
import jax.numpy as jnp
from jax import lax
from jax.experimental import pallas as pl
from jax.experimental.pallas import tpu as pltpu
from jax.sharding import PartitionSpec as P

BLOCK = 128
TILE = 32
MESH = pl.DeviceIdType.MESH
DIRS = [
    (a, b, c)
    for a in (-1, 0, 1)
    for b in (-1, 0, 1)
    for c in (-1, 0, 1)
    if (a, b, c) != (0, 0, 0)
]
PLANE = [(b, c) for b in (-1, 0, 1) for c in (-1, 0, 1) if (b, c) != (0, 0)]


def number(a, b, c):
    return DIRS.index((a, b, c))


def kernel(
    sizes,
    widths,
    map_ref,
    schur_hbm,
    vec_hbm,
    asm_hbm,
    upd_hbm,
    schur,
    vec,
    own_w,
    relay_w,
    maps,
    map_out,
    map_in,
    pays,
    parts,
    stages,
    recvs,
    comb,
    comb_in,
    tots,
    scaleds,
    asms,
    upds,
    load_sem,
    store_sem,
    mapc_sem,
    map_send,
    map_recv,
    x_send,
    x_recv,
    p_send,
    p_recv,
    b_send,
    b_recv,
):
    gx, gy, gz = sizes
    order = schur.shape[0]
    blocks = order // BLOCK
    group_rows = 2 * BLOCK
    groups = order // group_rows
    last = len(widths) - 1
    p, q, r = lax.axis_index("gx"), lax.axis_index("gy"), lax.axis_index("gz")
    shifts = (1,) if gx == 2 else (-1, 1)

    def slot(a):
        return 0 if gx == 2 or a == -1 else 1

    def inside(b, c):
        return (q + b >= 0) & (q + b < gy) & (r + c >= 0) & (r + c < gz)

    def across(a):
        return {"gx": lax.rem(p + a + gx, gx), "gy": q, "gz": r}

    def beside(b, c):
        return {"gx": p, "gy": q + b, "gz": r + c}

    barrier = pltpu.get_barrier_semaphore()
    for a in shifts:
        pl.semaphore_signal(barrier, inc=1, device_id=across(a), device_id_type=MESH)
    for b, c in PLANE:

        @pl.when(inside(b, c))
        def _(b=b, c=c):
            pl.semaphore_signal(barrier, inc=1, device_id=beside(b, c), device_id_type=MESH)

    rows_near = 3 - jnp.where(q == 0, 1, 0) - jnp.where(q == gy - 1, 1, 0)
    cols_near = 3 - jnp.where(r == 0, 1, 0) - jnp.where(r == gz - 1, 1, 0)
    peers = rows_near * cols_near - 1 + len(shifts)

    vec_copy = pltpu.make_async_copy(vec_hbm, vec, load_sem.at[groups])
    vec_copy.start()
    loads = []
    for g in range(groups):
        rows = pl.ds(g * group_rows, group_rows)
        load = pltpu.make_async_copy(schur_hbm.at[rows], schur.at[rows], load_sem.at[g])
        load.start()
        loads.append(load)

    lanes = lax.broadcasted_iota(jnp.int32, (8, 128), 1)
    row = jnp.zeros((8, 128), jnp.int32)
    for e in range(26):
        row = jnp.where(lanes == e, map_ref[e], row)
    map_out[...] = row

    for e, (a, b, c) in enumerate(DIRS):
        alive = inside(-b, -c)
        for k in range(blocks):
            hit = (map_ref[25 - e] == k) & alive
            own_w[e * blocks + k] = jnp.where(hit, 1.0, 0.0).astype(jnp.float32)
    for s, (b, c) in enumerate(PLANE):

        @pl.when(jnp.logical_not(inside(-b, -c)))
        def _(s=s):
            for recv in recvs:
                recv[s] = jnp.zeros(recv.shape[1:], recv.dtype)

    def x_copy(j, a, lo, n, sem):
        return pltpu.make_async_remote_copy(
            src_ref=pays[j].at[pl.ds(lo, n)],
            dst_ref=parts[j].at[slot(a), pl.ds(lo, n)],
            send_sem=x_send.at[j, slot(a), sem],
            recv_sem=x_recv.at[j, slot(a), sem],
            device_id=across(a),
            device_id_type=MESH,
        )

    def map_copy(a):
        return pltpu.make_async_remote_copy(
            src_ref=map_out,
            dst_ref=map_in.at[slot(a)],
            send_sem=map_send.at[slot(a)],
            recv_sem=map_recv.at[slot(a)],
            device_id=across(a),
            device_id_type=MESH,
        )

    def plane_copy(j, s):
        b, c = PLANE[s]
        return pltpu.make_async_remote_copy(
            src_ref=stages[j].at[s],
            dst_ref=recvs[j].at[s],
            send_sem=p_send.at[j, s],
            recv_sem=p_recv.at[j, s],
            device_id=beside(b, c),
            device_id_type=MESH,
        )

    def b_copy(a):
        return pltpu.make_async_remote_copy(
            src_ref=comb.at[slot(a)],
            dst_ref=comb_in.at[slot(a)],
            send_sem=b_send.at[slot(a)],
            recv_sem=b_recv.at[slot(a)],
            device_id=across(a),
            device_id_type=MESH,
        )

    vec_copy.wait()
    for g in range(groups):
        loads[g].wait()
        rows = pl.ds(g * group_rows, group_rows)
        product = jnp.dot(schur[rows, :], vec[...], preferred_element_type=jnp.float32)
        product = product.astype(jnp.bfloat16)
        for half in range(2):
            k = 2 * g + half
            part = product[half * BLOCK : (half + 1) * BLOCK]
            spot = pl.ds(k * BLOCK, BLOCK)
            pays[0][k, :, :BLOCK] = schur[spot, spot]
            start = 0
            for j, width in enumerate(widths):
                lead = BLOCK if j == 0 else 0
                pays[j][k, :, lead:] = part[:, start : start + width - lead]
                start += width - lead
        if g == 0:
            pl.semaphore_wait(barrier, peers)

            for a in shifts:
                map_copy(a).start()
        for a in shifts:
            x_copy(0, a, 2 * g, 2, g).start()
    for j in range(1, last):
        for a in shifts:
            x_copy(j, a, 0, blocks, 0).start()

    def stage(j, near):
        for s, (b, c) in enumerate(PLANE):

            @pl.when(inside(b, c))
            def _(s=s, b=b, c=c):
                stages[j][s, 1] = pays[j][map_ref[number(0, b, c)]]
                for place, a in ((0, -1), (2, 1)):
                    if near:
                        stages[j][s, place] = parts[j][
                            slot(a), maps[slot(a), 0, number(a, b, c)]
                        ]
                    else:
                        stages[j][s, place] = pays[j][map_ref[number(a, b, c)]]
                plane_copy(j, s).start()

    def arrived(j):
        for s, (b, c) in enumerate(PLANE):

            @pl.when(inside(-b, -c))
            def _(s=s):
                plane_copy(j, s).wait_recv()

    def accumulate(width, base, messages, store):
        per_row = width // BLOCK

        def step(t, carry):
            rows = pl.ds(pl.multiple_of(t // per_row * TILE, TILE), TILE)
            cols = pl.ds(pl.multiple_of(t % per_row * BLOCK, BLOCK), BLOCK)
            sums = [base(k, rows, cols) for k in range(blocks)]
            for read, weight in messages:
                value = read(rows, cols).astype(jnp.float32)
                for k in range(blocks):
                    term = value * weight(k)
                    sums[k] = term if sums[k] is None else sums[k] + term
            for k in range(blocks):
                store(k, rows, cols, sums[k])
            return carry

        lax.fori_loop(0, BLOCK // TILE * per_row, step, 0)

    def from_recv(j, s, place):
        return lambda rows, cols: recvs[j][s, place, rows, cols]

    def own_weight(e):
        return lambda k: own_w[e * blocks + k]

    def totals(j, terms):
        def base(k, rows, cols):
            return pays[j][k, rows, cols].astype(jnp.float32)

        def store(k, rows, cols, value):
            tots[j][k, rows, cols] = value

        messages = []
        for a in terms:
            for s, (b, c) in enumerate(PLANE):
                messages.append((from_recv(j, s, a + 1), own_weight(number(a, b, c))))
            if a != 0:

                def read(rows, cols, a=a):
                    return parts[j][slot(a), maps[slot(a), 0, number(a, 0, 0)], rows, cols]

                messages.append((read, own_weight(number(a, 0, 0))))
        accumulate(widths[j], base, messages, store)

    stage(last, False)

    for a in shifts:
        map_copy(a).wait_recv()
        mover = pltpu.make_async_copy(map_in.at[slot(a)], maps.at[slot(a)], mapc_sem.at[slot(a)])
        mover.start()
        mover.wait()
    for a in (-1, 1):
        for b in (-1, 0, 1):
            for c in (-1, 0, 1):
                e = number(a, b, c)
                alive = inside(-b, -c)
                for k in range(blocks):
                    hit = (maps[slot(-a), 0, 25 - e] == k) & alive
                    relay_w[e * blocks + k] = jnp.where(hit, 1.0, 0.0).astype(jnp.float32)

    for a in shifts:
        for g in range(groups):
            x_copy(0, a, 2 * g, 2, g).wait_recv()
    stage(0, True)

    arrived(last)
    for target in shifts:
        messages = []
        for a in (-1, 1):
            if slot(a) != slot(target):
                continue
            for s, (b, c) in enumerate(PLANE):
                e = number(a, b, c)
                messages.append((from_recv(last, s, a + 1), lambda k, e=e: relay_w[e * blocks + k]))
            e = number(a, 0, 0)

            def read(rows, cols, e=e):
                return pays[last][map_ref[e], rows, cols]

            messages.append((read, lambda k, e=e: relay_w[e * blocks + k]))

        def store(k, rows, cols, value, target=target):
            comb[slot(target), k, rows, cols] = value.astype(jnp.bfloat16)

        accumulate(widths[last], lambda k, rows, cols: None, messages, store)
        b_copy(target).start()

    for j in range(1, last):
        for a in shifts:
            x_copy(j, a, 0, blocks, 0).wait_recv()
        stage(j, True)
    totals(last, (0,))

    counts = []
    for k in range(blocks):
        count = jnp.float32(1.0)
        for e in range(26):
            count = count + own_w[e * blocks + k]
        counts.append(count)

    stores = []

    def finish(j, start):
        lead = BLOCK if j == 0 else 0
        width = widths[j] - lead
        for k in range(blocks):
            summed = tots[j][k, :, lead:]
            if j == last:
                for a in shifts:
                    summed = summed + comb_in[slot(a), k].astype(jnp.float32)
            spot = pl.ds(k * BLOCK, BLOCK)
            value = jnp.dot(
                tots[0][k, :, :BLOCK],
                summed,
                precision=lax.Precision.HIGHEST,
                preferred_element_type=jnp.float32,
            )
            scaleds[j][spot, :] = (value / counts[k]).astype(jnp.bfloat16)
            asms[j][spot, :] = summed.astype(jnp.bfloat16)
        cols = pl.ds(start, width)
        out = pltpu.make_async_copy(asms[j], asm_hbm.at[:, cols], store_sem.at[0, j])
        out.start()
        stores.append(out)

        def step(t, carry):
            rows = pl.ds(pl.multiple_of(t * group_rows, group_rows), group_rows)
            upds[j][rows, :] = jnp.dot(
                schur[rows, :], scaleds[j][...], preferred_element_type=jnp.float32
            ).astype(jnp.bfloat16)
            return carry

        lax.fori_loop(0, groups, step, 0)
        out = pltpu.make_async_copy(upds[j], upd_hbm.at[:, cols], store_sem.at[1, j])
        out.start()
        stores.append(out)
        return start + width

    start = 0
    for j in range(last):
        arrived(j)
        totals(j, (-1, 0, 1))
        start = finish(j, start)
    for a in shifts:
        b_copy(a).wait_recv()
    finish(last, start)

    for a in shifts:
        map_copy(a).wait_send()
        for g in range(groups):
            x_copy(0, a, 2 * g, 2, g).wait_send()
        for j in range(1, last):
            x_copy(j, a, 0, blocks, 0).wait_send()
        b_copy(a).wait_send()
    for s, (b, c) in enumerate(PLANE):

        @pl.when(inside(b, c))
        def _(s=s):
            for j in range(last + 1):
                plane_copy(j, s).wait_send()

    for out in stores:
        out.wait()


def local(sizes, schur, block_map, vectors):
    matrix = schur[0, 0, 0]
    right_side = vectors[0, 0, 0]
    links = block_map[0, 0, 0]
    order, rhs = right_side.shape
    blocks = order // BLOCK
    groups = order // (2 * BLOCK)
    bf16, f32, i32 = jnp.bfloat16, jnp.float32, jnp.int32
    widths = (2 * BLOCK, rhs // 2 - BLOCK, rhs // 2)
    chunks = len(widths)
    near = 1 if sizes[0] == 2 else 2
    clean = (widths[0] - BLOCK,) + widths[1:]
    vmem, dma = pltpu.VMEM, pltpu.SemaphoreType.DMA
    scratch = [
        vmem((order, order), bf16),
        vmem((order, rhs), bf16),
        pltpu.SMEM((26 * blocks,), f32),
        pltpu.SMEM((26 * blocks,), f32),
        pltpu.SMEM((near, 8, 128), i32),
        vmem((8, 128), i32),
        vmem((near, 8, 128), i32),
        [vmem((blocks, BLOCK, w), bf16) for w in widths],
        [vmem((near, blocks, BLOCK, w), bf16) for w in widths[:-1]],
        [vmem((8, 3, BLOCK, w), bf16) for w in widths],
        [vmem((8, 3, BLOCK, w), bf16) for w in widths],
        vmem((near, blocks, BLOCK, widths[-1]), bf16),
        vmem((near, blocks, BLOCK, widths[-1]), bf16),
        [vmem((blocks, BLOCK, w), f32) for w in widths],
        [vmem((order, w), bf16) for w in clean],
        [vmem((order, w), bf16) for w in clean],
        [vmem((order, w), bf16) for w in clean],
        dma((groups + 1,)),
        dma((2, chunks)),
        dma((near,)),
        dma((near,)),
        dma((near,)),
        dma((chunks - 1, near, groups)),
        dma((chunks - 1, near, groups)),
        dma((chunks, 8)),
        dma((chunks, 8)),
        dma((near,)),
        dma((near,)),
    ]
    anywhere = pl.BlockSpec(memory_space=pl.ANY)
    assembled, update = pl.pallas_call(
        functools.partial(kernel, sizes, widths),
        out_shape=[jax.ShapeDtypeStruct((order, rhs), bf16)] * 2,
        in_specs=[pl.BlockSpec(memory_space=pltpu.SMEM), anywhere, anywhere],
        out_specs=[anywhere, anywhere],
        scratch_shapes=scratch,
        compiler_params=pltpu.CompilerParams(
            collective_id=0, has_side_effects=True, vmem_limit_bytes=60 * 1024 * 1024
        ),
    )(links, matrix, right_side)
    return assembled[None, None, None], update[None, None, None]


def solution(mesh):
    placed = (
        P("gx", "gy", "gz", None, None),
        P("gx", "gy", "gz", None),
        P("gx", "gy", "gz", None, None),
    )
    sizes = tuple(mesh.shape[name] for name in ("gx", "gy", "gz"))
    return jax.shard_map(
        functools.partial(local, sizes),
        mesh=mesh,
        in_specs=placed,
        out_specs=(P("gx", "gy", "gz", None, None), P("gx", "gy", "gz", None, None)),
        check_vma=False,
    )
```

time: 136 us -> 46.6 us (0.34)
  the two profiles are of different devices: /device:TPU:17 before, /device:TPU:1 now
where the time goes in v1:
time: 46.6 us; the launch traced here: 45.8 us
  Pallas kernels  41.8 us (90%)
  local copies, waits for them, and re-layouts  3.32 us (7%)
  between operations  0.65 us (1%)
    pallas_call x1, Pallas kernels, local(): pl.pallas_call(functools.partial(kernel, sizes, widths), out_shape=[jax.S...  41.8 us
    unnamed x4, local copies, waits for them, and re-layouts  3.32 us

profile of v1, /device:TPU:1, one launch (start us, length us, event | category | flops | bytes accessed | tf_op | source)
XLA Modules:
  0.0 45.8 jit_solution(16666761422767172465)
XLA Ops:
  0.6 41.8 %shard_map.50 = (bf16[1024,512]{1,0:T(8,128)(2,1)}, bf16[1024,512]{1,0:T(8,128)(2,1)}) custom-call(s32[26]{0:T(128)} %bitcast.9, bf16[1024,1024]{1,0:T(8,128)(2,1)} %bitcast.5, bf16[1024,512]{1,0:T(8,128)(2,1)} %bitcast.6), custom_call_target="tpu_custom_call" | custom-call | tf_op jit(solution)/shard_map/pallas_call | solution.py:422
  42.4 0.0 copy-start
  42.5 2.4 %copy.7 = bf16[1,1,1,1024,512]{4,3,2,1,0:T(8,128)(2,1)} copy(bf16[1,1,1,1024,512]{4,3,2,1,0:T(8,128)(2,1)} %bitcast.8) | data formatting | bytes 2097152
  44.8 0.0 copy-done
  44.8 1.0 %copy.8 = bf16[1,1,1,1024,512]{4,3,2,1,0:T(8,128)(2,1)} copy(bf16[1,1,1,1024,512]{4,3,2,1,0:T(8,128)(2,1)S(1)} %bitcast.7) | data formatting | bytes 2097152
Async XLA Ops:
  42.4 2.4 %copy-start = (bf16[1024,512]{1,0:T(8,128)(2,1)S(1)}, bf16[1024,512]{1,0:T(8,128)(2,1)}, u32[]{:S(2)}) copy-start(bf16[1024,512]{1,0:T(8,128)(2,1)} %get-tuple-element.5) | copy-start | bytes 3145732

commit v2 on v1

--- a/solution.py
+++ b/solution.py
@@ -27,6 +27,7 @@
 def kernel(
     sizes,
     widths,
+    starts,
     map_ref,
     schur_hbm,
     vec_hbm,
@@ -46,9 +47,11 @@
     comb,
     comb_in,
     tots,
+    coupling,
     scaleds,
     asms,
     upds,
+    tile_sem,
     load_sem,
     store_sem,
     mapc_sem,
@@ -66,7 +69,7 @@
     blocks = order // BLOCK
     group_rows = 2 * BLOCK
     groups = order // group_rows
-    last = len(widths) - 1
+    far = (3, 4)
     p, q, r = lax.axis_index("gx"), lax.axis_index("gy"), lax.axis_index("gz")
     shifts = (1,) if gx == 2 else (-1, 1)
 
@@ -95,6 +98,12 @@
     cols_near = 3 - jnp.where(r == 0, 1, 0) - jnp.where(r == gz - 1, 1, 0)
     peers = rows_near * cols_near - 1 + len(shifts)
 
+    tiles = []
+    for k in range(blocks):
+        spot = pl.ds(k * BLOCK, BLOCK)
+        tile = pltpu.make_async_copy(schur_hbm.at[spot, spot], pays[0].at[k], tile_sem.at[k])
+        tile.start()
+        tiles.append(tile)
     vec_copy = pltpu.make_async_copy(vec_hbm, vec, load_sem.at[groups])
     vec_copy.start()
     loads = []
@@ -153,15 +162,22 @@
             device_id_type=MESH,
         )
 
-    def b_copy(a):
+    def b_copy(i, a):
         return pltpu.make_async_remote_copy(
-            src_ref=comb.at[slot(a)],
-            dst_ref=comb_in.at[slot(a)],
-            send_sem=b_send.at[slot(a)],
-            recv_sem=b_recv.at[slot(a)],
+            src_ref=comb.at[i, slot(a)],
+            dst_ref=comb_in.at[i, slot(a)],
+            send_sem=b_send.at[i, slot(a)],
+            recv_sem=b_recv.at[i, slot(a)],
             device_id=across(a),
             device_id_type=MESH,
         )
+
+    for tile in tiles:
+        tile.wait()
+    pl.semaphore_wait(barrier, peers)
+    for a in shifts:
+        map_copy(a).start()
+        x_copy(0, a, 0, blocks, 0).start()
 
     vec_copy.wait()
     for g in range(groups):
@@ -170,25 +186,14 @@
         product = jnp.dot(schur[rows, :], vec[...], preferred_element_type=jnp.float32)
         product = product.astype(jnp.bfloat16)
         for half in range(2):
-            k = 2 * g + half
-            part = product[half * BLOCK : (half + 1) * BLOCK]
-            spot = pl.ds(k * BLOCK, BLOCK)
-            pays[0][k, :, :BLOCK] = schur[spot, spot]
-            start = 0
-            for j, width in enumerate(widths):
-                lead = BLOCK if j == 0 else 0
-                pays[j][k, :, lead:] = part[:, start : start + width - lead]
-                start += width - lead
-        if g == 0:
-            pl.semaphore_wait(barrier, peers)
-
-            for a in shifts:
-                map_copy(a).start()
+            for j in range(1, len(widths)):
+                pays[j][2 * g + half] = product[
+                    half * BLOCK : (half + 1) * BLOCK, starts[j] : starts[j] + widths[j]
+                ]
         for a in shifts:
-            x_copy(0, a, 2 * g, 2, g).start()
-    for j in range(1, last):
-        for a in shifts:
-            x_copy(j, a, 0, blocks, 0).start()
+            x_copy(1, a, 2 * g, 2, g).start()
+    for a in shifts:
+        x_copy(2, a, 0, blocks, 0).start()
 
     def stage(j, near):
         for s, (b, c) in enumerate(PLANE):
@@ -255,7 +260,8 @@
                 messages.append((read, own_weight(number(a, 0, 0))))
         accumulate(widths[j], base, messages, store)
 
-    stage(last, False)
+    for j in far:
+        stage(j, False)
 
     for a in shifts:
         map_copy(a).wait_recv()
@@ -271,38 +277,46 @@
                     hit = (maps[slot(-a), 0, 25 - e] == k) & alive
                     relay_w[e * blocks + k] = jnp.where(hit, 1.0, 0.0).astype(jnp.float32)
 
+    def relay(j):
+        i = far.index(j)
+        arrived(j)
+        for target in shifts:
+            messages = []
+            for a in (-1, 1):
+                if slot(a) != slot(target):
+                    continue
+                for s, (b, c) in enumerate(PLANE):
+                    e = number(a, b, c)
+                    messages.append(
+                        (from_recv(j, s, a + 1), lambda k, e=e: relay_w[e * blocks + k])
+                    )
+                e = number(a, 0, 0)
+
+                def read(rows, cols, e=e):
+                    return pays[j][map_ref[e], rows, cols]
+
+                messages.append((read, lambda k, e=e: relay_w[e * blocks + k]))
+
+            def store(k, rows, cols, value, target=target):
+                comb[i, slot(target), k, rows, cols] = value.astype(jnp.bfloat16)
+
+            accumulate(widths[j], lambda k, rows, cols: None, messages, store)
+            b_copy(i, target).start()
+
+    for a in shifts:
+        x_copy(0, a, 0, blocks, 0).wait_recv()
+    stage(0, True)
+    relay(far[0])
     for a in shifts:
         for g in range(groups):
-            x_copy(0, a, 2 * g, 2, g).wait_recv()
-    stage(0, True)
-
-    arrived(last)
-    for target in shifts:
-        messages = []
-        for a in (-1, 1):
-            if slot(a) != slot(target):
-                continue
-            for s, (b, c) in enumerate(PLANE):
-                e = number(a, b, c)
-                messages.append((from_recv(last, s, a + 1), lambda k, e=e: relay_w[e * blocks + k]))
-            e = number(a, 0, 0)
-
-            def read(rows, cols, e=e):
-                return pays[last][map_ref[e], rows, cols]
-
-            messages.append((read, lambda k, e=e: relay_w[e * blocks + k]))
-
-        def store(k, rows, cols, value, target=target):
-            comb[slot(target), k, rows, cols] = value.astype(jnp.bfloat16)
-
-        accumulate(widths[last], lambda k, rows, cols: None, messages, store)
-        b_copy(target).start()
-
-    for j in range(1, last):
-        for a in shifts:
-            x_copy(j, a, 0, blocks, 0).wait_recv()
-        stage(j, True)
-    totals(last, (0,))
+            x_copy(1, a, 2 * g, 2, g).wait_recv()
+    stage(1, True)
+    relay(far[1])
+    totals(far[0], (0,))
+    for a in shifts:
+        x_copy(2, a, 0, blocks, 0).wait_recv()
+    stage(2, True)
+    totals(far[1], (0,))
 
     counts = []
     for k in range(blocks):
@@ -311,64 +325,73 @@
             count = count + own_w[e * blocks + k]
         counts.append(count)
 
+    def split(value):
+        high = value.astype(jnp.bfloat16)
+        low = (value - high.astype(jnp.float32)).astype(jnp.bfloat16)
+        return high, low
+
+    arrived(0)
+    totals(0, (-1, 0, 1))
+    for k in range(blocks):
+        high, low = split(tots[0][k])
+        coupling[k, :, :BLOCK] = high
+        coupling[k, :, BLOCK:] = low
+
     stores = []
-
-    def finish(j, start):
-        lead = BLOCK if j == 0 else 0
-        width = widths[j] - lead
+    for i, (j, jj) in enumerate(((1, far[0]), (2, far[1]))):
+        arrived(j)
+        totals(j, (-1, 0, 1))
+        for a in shifts:
+            b_copy(i, a).wait_recv()
+        width = widths[j]
         for k in range(blocks):
-            summed = tots[j][k, :, lead:]
-            if j == last:
-                for a in shifts:
-                    summed = summed + comb_in[slot(a), k].astype(jnp.float32)
+            far_sum = tots[jj][k]
+            for a in shifts:
+                far_sum = far_sum + comb_in[i, slot(a), k].astype(jnp.float32)
+            summed = jnp.concatenate([tots[j][k], far_sum], axis=1)
+            high, low = split(summed)
             spot = pl.ds(k * BLOCK, BLOCK)
             value = jnp.dot(
-                tots[0][k, :, :BLOCK],
-                summed,
-                precision=lax.Precision.HIGHEST,
+                coupling[k],
+                jnp.concatenate([high, high], axis=0),
+                preferred_element_type=jnp.float32,
+            ) + jnp.dot(
+                coupling[k],
+                jnp.concatenate([low, low], axis=0),
                 preferred_element_type=jnp.float32,
             )
-            scaleds[j][spot, :] = (value / counts[k]).astype(jnp.bfloat16)
-            asms[j][spot, :] = summed.astype(jnp.bfloat16)
-        cols = pl.ds(start, width)
-        out = pltpu.make_async_copy(asms[j], asm_hbm.at[:, cols], store_sem.at[0, j])
+            scaleds[i][spot, :] = (value / counts[k]).astype(jnp.bfloat16)
+            asms[i][spot, :] = high
+        cols = pl.ds(starts[j], 2 * width)
+        out = pltpu.make_async_copy(asms[i], asm_hbm.at[:, cols], store_sem.at[0, i])
         out.start()
         stores.append(out)
 
-        def step(t, carry):
+        def step(t, carry, i=i):
             rows = pl.ds(pl.multiple_of(t * group_rows, group_rows), group_rows)
-            upds[j][rows, :] = jnp.dot(
-                schur[rows, :], scaleds[j][...], preferred_element_type=jnp.float32
+            upds[i][rows, :] = jnp.dot(
+                schur[rows, :], scaleds[i][...], preferred_element_type=jnp.float32
             ).astype(jnp.bfloat16)
             return carry
 
         lax.fori_loop(0, groups, step, 0)
-        out = pltpu.make_async_copy(upds[j], upd_hbm.at[:, cols], store_sem.at[1, j])
+        out = pltpu.make_async_copy(upds[i], upd_hbm.at[:, cols], store_sem.at[1, i])
         out.start()
         stores.append(out)
-        return start + width
-
-    start = 0
-    for j in range(last):
-        arrived(j)
-        totals(j, (-1, 0, 1))
-        start = finish(j, start)
-    for a in shifts:
-        b_copy(a).wait_recv()
-    finish(last, start)
 
     for a in shifts:
         map_copy(a).wait_send()
+        x_copy(0, a, 0, blocks, 0).wait_send()
         for g in range(groups):
-            x_copy(0, a, 2 * g, 2, g).wait_send()
-        for j in range(1, last):
-            x_copy(j, a, 0, blocks, 0).wait_send()
-        b_copy(a).wait_send()
+            x_copy(1, a, 2 * g, 2, g).wait_send()
+        x_copy(2, a, 0, blocks, 0).wait_send()
+        for i in range(2):
+            b_copy(i, a).wait_send()
     for s, (b, c) in enumerate(PLANE):
 
         @pl.when(inside(b, c))
         def _(s=s):
-            for j in range(last + 1):
+            for j in range(len(widths)):
                 plane_copy(j, s).wait_send()
 
     for out in stores:
@@ -383,10 +406,11 @@
     blocks = order // BLOCK
     groups = order // (2 * BLOCK)
     bf16, f32, i32 = jnp.bfloat16, jnp.float32, jnp.int32
-    widths = (2 * BLOCK, rhs // 2 - BLOCK, rhs // 2)
+    share = rhs // 4
+    widths = (BLOCK, share, share, share, share)
+    starts = (0, 0, 2 * share, share, 3 * share)
     chunks = len(widths)
     near = 1 if sizes[0] == 2 else 2
-    clean = (widths[0] - BLOCK,) + widths[1:]
     vmem, dma = pltpu.VMEM, pltpu.SemaphoreType.DMA
     scratch = [
         vmem((order, order), bf16),
@@ -397,30 +421,32 @@
         vmem((8, 128), i32),
         vmem((near, 8, 128), i32),
         [vmem((blocks, BLOCK, w), bf16) for w in widths],
-        [vmem((near, blocks, BLOCK, w), bf16) for w in widths[:-1]],
+        [vmem((near, blocks, BLOCK, w), bf16) for w in widths[:3]],
         [vmem((8, 3, BLOCK, w), bf16) for w in widths],
         [vmem((8, 3, BLOCK, w), bf16) for w in widths],
-        vmem((near, blocks, BLOCK, widths[-1]), bf16),
-        vmem((near, blocks, BLOCK, widths[-1]), bf16),
+        vmem((2, near, blocks, BLOCK, share), bf16),
+        vmem((2, near, blocks, BLOCK, share), bf16),
         [vmem((blocks, BLOCK, w), f32) for w in widths],
-        [vmem((order, w), bf16) for w in clean],
-        [vmem((order, w), bf16) for w in clean],
-        [vmem((order, w), bf16) for w in clean],
+        vmem((blocks, BLOCK, 2 * BLOCK), bf16),
+        [vmem((order, 2 * share), bf16) for _ in range(2)],
+        [vmem((order, 2 * share), bf16) for _ in range(2)],
+        [vmem((order, 2 * share), bf16) for _ in range(2)],
+        dma((blocks,)),
         dma((groups + 1,)),
-        dma((2, chunks)),
+        dma((2, 2)),
         dma((near,)),
         dma((near,)),
         dma((near,)),
-        dma((chunks - 1, near, groups)),
-        dma((chunks - 1, near, groups)),
+        dma((3, near, groups)),
+        dma((3, near, groups)),
         dma((chunks, 8)),
         dma((chunks, 8)),
-        dma((near,)),
-        dma((near,)),
+        dma((2, near)),
+        dma((2, near)),
     ]
     anywhere = pl.BlockSpec(memory_space=pl.ANY)
     assembled, update = pl.pallas_call(
-        functools.partial(kernel, sizes, widths),
+        functools.partial(kernel, sizes, widths, starts),
         out_shape=[jax.ShapeDtypeStruct((order, rhs), bf16)] * 2,
         in_specs=[pl.BlockSpec(memory_space=pltpu.SMEM), anywhere, anywhere],
         out_specs=[anywhere, anywhere],

time: 46.6 us -> 42.7 us (0.916); the launches traced: 45.8 us -> 42.6 us
  Pallas kernels: 41.8 us -> 38.6 us
    pallas_call x1, Pallas kernels: 41.8 us -> 38.6 us  [local(): pl.pallas_call(functools.partial(kernel, sizes, widths, starts), out_shap...]
where the time goes in v2:
time: 42.7 us; the launch traced here: 42.6 us
  Pallas kernels  38.6 us (90%)
  local copies, waits for them, and re-layouts  3.32 us (8%)
  between operations  0.65 us (2%)
    pallas_call x1, Pallas kernels, local(): pl.pallas_call(functools.partial(kernel, sizes, widths, starts), out_shap...  38.6 us
    unnamed x4, local copies, waits for them, and re-layouts  3.32 us

profile of v2, /device:TPU:1, one launch (start us, length us, event | category | flops | bytes accessed | tf_op | source)
XLA Modules:
  0.0 42.6 jit_solution(9824852266340150269)
XLA Ops:
  0.6 38.6 %shard_map.50 = (bf16[1024,512]{1,0:T(8,128)(2,1)}, bf16[1024,512]{1,0:T(8,128)(2,1)}) custom-call(s32[26]{0:T(128)} %bitcast.9, bf16[1024,1024]{1,0:T(8,128)(2,1)} %bitcast.5, bf16[1024,512]{1,0:T(8,128)(2,1)} %bitcast.6), custom_call_target="tpu_custom_call" | custom-call | tf_op jit(solution)/shard_map/pallas_call | solution.py:448
  39.2 0.0 copy-start
  39.2 2.4 %copy.7 = bf16[1,1,1,1024,512]{4,3,2,1,0:T(8,128)(2,1)} copy(bf16[1,1,1,1024,512]{4,3,2,1,0:T(8,128)(2,1)} %bitcast.8) | data formatting | bytes 2097152
  41.6 0.0 copy-done
  41.6 1.0 %copy.8 = bf16[1,1,1,1024,512]{4,3,2,1,0:T(8,128)(2,1)} copy(bf16[1,1,1,1024,512]{4,3,2,1,0:T(8,128)(2,1)S(1)} %bitcast.7) | data formatting | bytes 2097152
Async XLA Ops:
  39.2 2.4 %copy-start = (bf16[1024,512]{1,0:T(8,128)(2,1)S(1)}, bf16[1024,512]{1,0:T(8,128)(2,1)}, u32[]{:S(2)}) copy-start(bf16[1024,512]{1,0:T(8,128)(2,1)} %get-tuple-element.5) | copy-start | bytes 3145732

commit v3 on v2

--- a/solution.py
+++ b/solution.py
@@ -452,7 +452,7 @@
         out_specs=[anywhere, anywhere],
         scratch_shapes=scratch,
         compiler_params=pltpu.CompilerParams(
-            collective_id=0, has_side_effects=True, vmem_limit_bytes=60 * 1024 * 1024
+            collective_id=0, has_side_effects=True, vmem_limit_bytes=51 * 1024 * 1024
         ),
     )(links, matrix, right_side)
     return assembled[None, None, None], update[None, None, None]

time: 42.7 us -> 41.2 us (0.965)
  Pallas kernels: 38.6 us -> 37.8 us
  local copies, waits for them, and re-layouts: 3.32 us -> 2.59 us
    pallas_call x1, Pallas kernels: 38.6 us -> 37.8 us  [local(): pl.pallas_call(functools.partial(kernel, sizes, widths, starts), out_shap...]
    unnamed x4, local copies, waits for them, and re-layouts: 3.32 us -> 2.59 us
where the time goes in v3:
time: 41.2 us; the launch traced here: 41 us
  Pallas kernels  37.8 us (92%)
  local copies, waits for them, and re-layouts  2.59 us (6%)
  between operations  0.65 us (2%)
    pallas_call x1, Pallas kernels, local(): pl.pallas_call(functools.partial(kernel, sizes, widths, starts), out_shap...  37.8 us
    unnamed x4, local copies, waits for them, and re-layouts  2.59 us

profile of v3, /device:TPU:1, one launch (start us, length us, event | category | flops | bytes accessed | tf_op | source)
XLA Modules:
  0.0 41.0 jit_solution(7262615163208103443)
XLA Ops:
  0.6 0.0 copy-start
  0.6 0.6 %copy-done = s32[1,1,1,26]{3,2,1,0:T(1,128)S(1)} copy-done((s32[1,1,1,26]{3,2,1,0:T(1,128)S(1)}, s32[1,1,1,26]{3,2,1,0:T(1,128)}, u32[]{:S(2)}) %copy-start) | copy-done | bytes 128
  1.3 37.8 %shard_map.50 = (bf16[1024,512]{1,0:T(8,128)(2,1)S(1)}, bf16[1024,512]{1,0:T(8,128)(2,1)S(1)}) custom-call(s32[26]{0:T(128)S(1)} %bitcast.7, bf16[1024,1024]{1,0:T(8,128)(2,1)} %bitcast.8, bf16[1024,512]{1,0:T(8,128)(2,1)} %bitcast.9), custom_call_target="tpu_custom_call" | custom-call | tf_op jit(solution)/shard_map/pallas_call | solution.py:448
  39.1 1.0 %copy.7 = bf16[1,1,1,1024,512]{4,3,2,1,0:T(8,128)(2,1)} copy(bf16[1,1,1,1024,512]{4,3,2,1,0:T(8,128)(2,1)S(1)} %bitcast.6) | data formatting | bytes 2097152
  40.1 1.0 %copy.8 = bf16[1,1,1,1024,512]{4,3,2,1,0:T(8,128)(2,1)} copy(bf16[1,1,1,1024,512]{4,3,2,1,0:T(8,128)(2,1)S(1)} %bitcast.5) | data formatting | bytes 2097152
Async XLA Ops:
  0.6 0.7 %copy-start = (s32[1,1,1,26]{3,2,1,0:T(1,128)S(1)}, s32[1,1,1,26]{3,2,1,0:T(1,128)}, u32[]{:S(2)}) copy-start(s32[1,1,1,26]{3,2,1,0:T(1,128)} %param.4) | copy-start | bytes 316

commit v4 on v3

--- a/solution.py
+++ b/solution.py
@@ -113,24 +113,6 @@
         load.start()
         loads.append(load)
 
-    lanes = lax.broadcasted_iota(jnp.int32, (8, 128), 1)
-    row = jnp.zeros((8, 128), jnp.int32)
-    for e in range(26):
-        row = jnp.where(lanes == e, map_ref[e], row)
-    map_out[...] = row
-
-    for e, (a, b, c) in enumerate(DIRS):
-        alive = inside(-b, -c)
-        for k in range(blocks):
-            hit = (map_ref[25 - e] == k) & alive
-            own_w[e * blocks + k] = jnp.where(hit, 1.0, 0.0).astype(jnp.float32)
-    for s, (b, c) in enumerate(PLANE):
-
-        @pl.when(jnp.logical_not(inside(-b, -c)))
-        def _(s=s):
-            for recv in recvs:
-                recv[s] = jnp.zeros(recv.shape[1:], recv.dtype)
-
     def x_copy(j, a, lo, n, sem):
         return pltpu.make_async_remote_copy(
             src_ref=pays[j].at[pl.ds(lo, n)],
@@ -176,8 +158,17 @@
         tile.wait()
     pl.semaphore_wait(barrier, peers)
     for a in shifts:
+        x_copy(0, a, 0, blocks, 0).start()
+
+
+    lanes = lax.broadcasted_iota(jnp.int32, (8, 128), 1)
+    row = jnp.zeros((8, 128), jnp.int32)
+    for e in range(26):
+        row = jnp.where(lanes == e, map_ref[e], row)
+    map_out[...] = row
+
+    for a in shifts:
         map_copy(a).start()
-        x_copy(0, a, 0, blocks, 0).start()
 
     vec_copy.wait()
     for g in range(groups):
@@ -210,8 +201,10 @@
                         stages[j][s, place] = pays[j][map_ref[number(a, b, c)]]
                 plane_copy(j, s).start()
 
-    def arrived(j):
+    def arrived(j, rows=(-1, 0, 1)):
         for s, (b, c) in enumerate(PLANE):
+            if b not in rows:
+                continue
 
             @pl.when(inside(-b, -c))
             def _(s=s):
@@ -241,8 +234,10 @@
     def own_weight(e):
         return lambda k: own_w[e * blocks + k]
 
-    def totals(j, terms):
+    def totals(j, terms, near=(-1, 0, 1)):
         def base(k, rows, cols):
+            if 0 not in near:
+                return tots[j][k, rows, cols]
             return pays[j][k, rows, cols].astype(jnp.float32)
 
         def store(k, rows, cols, value):
@@ -251,8 +246,9 @@
         messages = []
         for a in terms:
             for s, (b, c) in enumerate(PLANE):
-                messages.append((from_recv(j, s, a + 1), own_weight(number(a, b, c))))
-            if a != 0:
+                if b in near:
+                    messages.append((from_recv(j, s, a + 1), own_weight(number(a, b, c))))
+            if a != 0 and 0 in near:
 
                 def read(rows, cols, a=a):
                     return parts[j][slot(a), maps[slot(a), 0, number(a, 0, 0)], rows, cols]
@@ -262,6 +258,18 @@
 
     for j in far:
         stage(j, False)
+
+    for e, (a, b, c) in enumerate(DIRS):
+        alive = inside(-b, -c)
+        for k in range(blocks):
+            hit = (map_ref[25 - e] == k) & alive
+            own_w[e * blocks + k] = jnp.where(hit, 1.0, 0.0).astype(jnp.float32)
+    for s, (b, c) in enumerate(PLANE):
+
+        @pl.when(jnp.logical_not(inside(-b, -c)))
+        def _(s=s):
+            for recv in recvs:
+                recv[s] = jnp.zeros(recv.shape[1:], recv.dtype)
 
     for a in shifts:
         map_copy(a).wait_recv()
@@ -339,8 +347,9 @@
 
     stores = []
     for i, (j, jj) in enumerate(((1, far[0]), (2, far[1]))):
-        arrived(j)
-        totals(j, (-1, 0, 1))
+        for near in ((0,), (-1, 1)):
+            arrived(j, near)
+            totals(j, (-1, 0, 1), near)
         for a in shifts:
             b_copy(i, a).wait_recv()
         width = widths[j]

time: 41.2 us -> 41.1 us (level)
  no operation moved by 1% of the time
where the time goes in v4:
time: 41.1 us; the launch traced here: 40.7 us
  Pallas kernels  37.4 us (91%)
  local copies, waits for them, and re-layouts  2.59 us (6%)
  between operations  0.65 us (2%)
    pallas_call x1, Pallas kernels, local(): pl.pallas_call(functools.partial(kernel, sizes, widths, starts), out_shap...  37.4 us
    unnamed x4, local copies, waits for them, and re-layouts  2.59 us

profile of v4, /device:TPU:1, one launch (start us, length us, event | category | flops | bytes accessed | tf_op | source)
XLA Modules:
  0.0 40.7 jit_solution(7909441778151607396)
XLA Ops:
  0.6 0.0 copy-start
  0.6 0.6 %copy-done = s32[1,1,1,26]{3,2,1,0:T(1,128)S(1)} copy-done((s32[1,1,1,26]{3,2,1,0:T(1,128)S(1)}, s32[1,1,1,26]{3,2,1,0:T(1,128)}, u32[]{:S(2)}) %copy-start) | copy-done | bytes 128
  1.3 37.4 %shard_map.50 = (bf16[1024,512]{1,0:T(8,128)(2,1)S(1)}, bf16[1024,512]{1,0:T(8,128)(2,1)S(1)}) custom-call(s32[26]{0:T(128)S(1)} %bitcast.7, bf16[1024,1024]{1,0:T(8,128)(2,1)} %bitcast.8, bf16[1024,512]{1,0:T(8,128)(2,1)} %bitcast.9), custom_call_target="tpu_custom_call" | custom-call | tf_op jit(solution)/shard_map/pallas_call | solution.py:457
  38.7 1.0 %copy.7 = bf16[1,1,1,1024,512]{4,3,2,1,0:T(8,128)(2,1)} copy(bf16[1,1,1,1024,512]{4,3,2,1,0:T(8,128)(2,1)S(1)} %bitcast.6) | data formatting | bytes 2097152
  39.7 1.0 %copy.8 = bf16[1,1,1,1024,512]{4,3,2,1,0:T(8,128)(2,1)} copy(bf16[1,1,1,1024,512]{4,3,2,1,0:T(8,128)(2,1)S(1)} %bitcast.5) | data formatting | bytes 2097152
Async XLA Ops:
  0.6 0.7 %copy-start = (s32[1,1,1,26]{3,2,1,0:T(1,128)S(1)}, s32[1,1,1,26]{3,2,1,0:T(1,128)}, u32[]{:S(2)}) copy-start(s32[1,1,1,26]{3,2,1,0:T(1,128)} %param.4) | copy-start | bytes 316
